TPU v7x, 256 devices: a whole 4x4x8 slice. The times are simulated.
256 devices in a mesh: req: 64 (over x, z, core), tp: 4 (over y).
Axes of the slice: x: 4, y: 4, z: 8, core: 2. Of those that a mesh axis runs over, the one named last changes fastest.
Arguments:
- hidden_in: bfloat16 [512, 1600], P('req'), may hold values from -6 to 6
- norm_gain: float32 [1600], replicated, may hold values from 0.1 to 1.9
- query_weight: bfloat16 [1600, 1280], P(None, 'tp'), may hold values from -0.15625 to 0.15625
- memory_weight: bfloat16 [1600, 512], P(None, 'tp'), may hold values from -0.15625 to 0.15625
- attention_out: bfloat16 [1280, 1600], P('tp'), may hold values from -0.15625 to 0.15625
- attention_gain: float32 [1280], P('tp'), may hold values from 0.1 to 1.9
- mamba_input: bfloat16 [2, 1600, 1600], P(None, None, 'tp'), may hold values from -0.15625 to 0.15625
- conv_weight: float32 [4, 1600], P(None, 'tp'), may hold values from -3 to 3
- conv_state: bfloat16 [512, 3, 1600], P('req', None, 'tp'), may hold values from -6 to 6
- select_weight: bfloat16 [1600, 132], P('tp'), may hold values from -0.15625 to 0.15625
- step_weight: bfloat16 [100, 1600], P(None, 'tp'), may hold values from -0.625 to 0.625
- step_bias: float32 [1600], P('tp'), may hold values from -4 to -1
- decay_log: float32 [16, 1600], P(None, 'tp'), may hold values from 0 to 2.77
- skip_gain: float32 [1600], P('tp'), may hold values from 0.5 to 1.5
- scan_state: float32 [512, 16, 1600], P('req', None, 'tp'), may hold values from -6 to 6
- mamba_gain: float32 [1600], P('tp'), may hold values from 0.1 to 1.9
- mamba_out: bfloat16 [1600, 1600], P('tp'), may hold values from -0.15625 to 0.15625
- cache_blocks: bfloat16 [2176, 4, 512, 128], P('req', 'tp'), as said below
- lengths: int32 [512], replicated, may hold values from 257 to 8192, as said below
- slot_request: int32 [2176], P('req'), may hold values from -1 to 511, as said below
- slot_block: int32 [2176], P('req'), may hold values from 0 to 15, as said below
Outputs:
- layer_out: bfloat16 [512, 1600], P('req', 'tp')
- new_state: float32 [512, 16, 1600], P('req', None, 'tp')
Inputs may be any that keep to these rules, and one draw needn't show every extreme that they name: `lengths`: some request holds exactly 8192 tokens. `slot_request`: -1 marks an empty slot; a request with L cached tokens fills exactly ceil(L / 512) slots; the slots of one index of req hold at most 2 blocks of the requests of any one index of req (requests r with equal r // 8), and some index of req holds exactly 2. `slot_block`: the slots of one request carry its block numbers 0 to ceil(L / 512) - 1, each once; empty slots carry 0. `cache_blocks`: the first 64 entries of the last dimension are keys, the rest values.
All inputs are finite; a program needn't handle non-finite values.
Results may differ from a plain program's by a relative error of at most 0.012.
Values may be sent and summed in bfloat16 or wider, within the bound.
A program may use at most 64 MiB of HBM per device.

v0:
```python
import jax
import jax.numpy as jnp
from jax import lax
from jax.sharding import PartitionSpec as P

HQ = 20
HD = 64
MI = 1600


def rotate_pairs(vector, position):
    head_dim = vector.shape[-1]
    half_dim = head_dim // 2
    frequency = jnp.power(
        jnp.float32(10000.0), -jnp.arange(half_dim, dtype=jnp.float32) * (2.0 / head_dim)
    )
    angles = position.astype(jnp.float32)[:, None, None] * frequency
    cosine = jnp.cos(angles)
    sine_part = jnp.sin(angles)
    front_half = vector[..., :half_dim]
    back_half = vector[..., half_dim:]
    return jnp.concatenate(
        [front_half * cosine - back_half * sine_part, back_half * cosine + front_half * sine_part],
        -1,
    )


def body(
    hidden_in,
    norm_gain,
    query_weight,
    memory_weight,
    attention_out,
    attention_gain,
    mamba_input,
    conv_weight,
    conv_state,
    select_weight,
    step_weight,
    step_bias,
    decay_log,
    skip_gain,
    scan_state,
    mamba_gain,
    mamba_out,
    cache_blocks,
    lengths,
    slot_request,
    slot_block,
):
    row_count = hidden_in.shape[0]
    model_width = hidden_in.shape[1]
    head_dim = cache_blocks.shape[3] // 2
    head_count = query_weight.shape[1] // head_dim
    block_len = cache_blocks.shape[2]
    slot_count = cache_blocks.shape[0]
    request_count = lengths.shape[0]
    holders = lax.axis_size("req")
    tp_count = lax.axis_size("tp")
    own_first = lax.axis_index("req") * row_count
    own_len = lax.dynamic_slice_in_dim(lengths, own_first, row_count)
    hidden_f = hidden_in.astype(jnp.float32)
    normed = (
        hidden_f * lax.rsqrt(jnp.mean(hidden_f * hidden_f, -1, keepdims=True) + 1e-06) * norm_gain
    ).astype(jnp.bfloat16)
    query_raw = jnp.dot(normed, query_weight, preferred_element_type=jnp.float32).reshape(
        row_count, head_count, head_dim
    )
    query = rotate_pairs(query_raw, own_len).astype(jnp.bfloat16)
    memory = jnp.dot(normed, memory_weight, preferred_element_type=jnp.float32)
    key_new = rotate_pairs(memory[:, None, :head_dim], own_len).astype(jnp.bfloat16)
    value_new = memory[:, head_dim:].astype(jnp.bfloat16)
    all_query = lax.all_gather(
        query.reshape(row_count, head_count * head_dim), "req", axis=0, tiled=True
    )
    slot_used = slot_request >= 0
    owner_row = jnp.where(slot_used, slot_request, 0)
    slot_query = jnp.take(all_query, owner_row, axis=0).reshape(slot_count, head_count, head_dim)
    keys = cache_blocks[:, 0, :, :head_dim]
    values = cache_blocks[:, 0, :, head_dim:]
    valid_len = jnp.where(slot_used, jnp.take(lengths, owner_row) - slot_block * block_len, 0)
    live_mask = jnp.arange(block_len)[None, :] < valid_len[:, None]
    scores = jnp.einsum(
        "shd,std->sht", slot_query, keys, preferred_element_type=jnp.float32
    ) * head_dim ** (-0.5)
    scores = jnp.where(live_mask[:, None, :], scores, -1e30)
    block_max = jnp.max(scores, 2)
    weights = jnp.where(live_mask[:, None, :], jnp.exp(scores - block_max[..., None]), 0.0).astype(
        jnp.bfloat16
    )
    block_sum = jnp.sum(weights.astype(jnp.float32), 2)
    block_out = jnp.einsum("sht,std->shd", weights, values, preferred_element_type=jnp.float32)
    own_score = jnp.sum(query.astype(jnp.float32) * key_new.astype(jnp.float32), -1) * head_dim ** (
        -0.5
    )
    value_own = value_new.astype(jnp.float32)[:, None, :]
    owner_match = slot_request[:, None] == jnp.arange(request_count)[None, :]
    request_max = jnp.max(jnp.where(owner_match[:, :, None], block_max[:, None, :], -1e30), axis=0)
    owner_table = owner_match.astype(jnp.float32)
    rescale = jnp.exp(block_max - jnp.take(request_max, owner_row, axis=0))
    scaled_out = (block_out * rescale[..., None]).reshape(slot_count, head_count * head_dim)
    part_out = jnp.dot(owner_table.T, scaled_out, precision=lax.Precision.HIGHEST)
    part_sum = jnp.dot(owner_table.T, block_sum * rescale, precision=lax.Precision.HIGHEST)
    part_out, part_sum = (part_out, part_sum)
    got_out, got_sum, got_max = (
        lax.all_to_all(
            part_out.reshape(holders, row_count, head_count * head_dim),
            "req",
            split_axis=0,
            concat_axis=0,
            tiled=True,
        ),
        lax.all_to_all(
            part_sum.reshape(holders, row_count, head_count),
            "req",
            split_axis=0,
            concat_axis=0,
            tiled=True,
        ),
        lax.all_to_all(
            request_max.reshape(holders, row_count, head_count),
            "req",
            split_axis=0,
            concat_axis=0,
            tiled=True,
        ),
    )
    top = jnp.maximum(jnp.max(got_max, 0), own_score)
    source_weight = jnp.exp(got_max - top[None])
    numer = jnp.sum(
        got_out.reshape(holders, row_count, head_count, head_dim) * source_weight[..., None], 0
    )
    denom = jnp.sum(got_sum * source_weight, 0)
    own_weight = jnp.exp(own_score - top)
    numer = numer + own_weight[..., None] * value_own
    denom = denom + own_weight
    attention = (numer / denom[..., None]).reshape(row_count, head_count * head_dim)
    mamba_x = jnp.dot(normed, mamba_input[0], preferred_element_type=jnp.float32).astype(
        jnp.bfloat16
    )
    gate_branch = jnp.dot(normed, mamba_input[1], preferred_element_type=jnp.float32)
    taps = conv_weight.shape[0]
    conv_sum = conv_weight[taps - 1] * mamba_x.astype(jnp.float32)
    for tap_index in range(taps - 1):
        conv_sum = conv_sum + conv_weight[tap_index] * conv_state[:, tap_index].astype(jnp.float32)
    activated = jax.nn.silu(conv_sum).astype(jnp.bfloat16)
    selection = lax.psum(
        jnp.dot(activated, select_weight, preferred_element_type=jnp.float32), "tp"
    )
    rank_width = step_weight.shape[0]
    state_width = decay_log.shape[0]
    step_rank = selection[:, :rank_width].astype(jnp.bfloat16)
    input_map = selection[:, rank_width : rank_width + state_width]
    output_map = selection[:, rank_width + state_width :]
    step_size = jax.nn.softplus(
        jnp.dot(step_rank, step_weight, preferred_element_type=jnp.float32) + step_bias
    )
    active_f = activated.astype(jnp.float32)
    new_state = (
        jnp.exp(-step_size[:, None, :] * jnp.exp(decay_log)[None]) * scan_state
        + step_size[:, None, :] * input_map[:, :, None] * active_f[:, None, :]
    )
    mamba_y = (jnp.sum(output_map[:, :, None] * new_state, 1) + skip_gain * active_f) * jax.nn.silu(
        gate_branch
    )
    attn_square = jnp.sum(attention * attention, -1)
    mamba_square = jnp.sum(mamba_y * mamba_y, -1)
    attn_used = (attention * attention_gain).astype(jnp.bfloat16)
    mamba_used = (mamba_y * mamba_gain).astype(jnp.bfloat16)
    attn_proj = jnp.dot(attn_used, attention_out, preferred_element_type=jnp.float32)
    mamba_proj = jnp.dot(mamba_used, mamba_out, preferred_element_type=jnp.float32)
    attn_total, mamba_total = lax.psum((attn_square, mamba_square), "tp")
    attn_scale = jnp.sqrt(attn_total / (HQ * HD) + 1e-06)
    mamba_scale = jnp.sqrt(mamba_total / MI + 1e-06)
    partial_value = 0.5 * (attn_proj / attn_scale[:, None] + mamba_proj / mamba_scale[:, None])
    mixed = lax.psum_scatter(partial_value, "tp", scatter_dimension=1, tiled=True)
    column_width = model_width // tp_count
    residual = lax.dynamic_slice_in_dim(
        hidden_f, lax.axis_index("tp") * column_width, column_width, 1
    )
    layer_out = (residual + mixed).astype(jnp.bfloat16)
    return (layer_out, new_state)


def solution(mesh):
    return jax.shard_map(
        body,
        mesh=mesh,
        in_specs=(
            P("req", None),
            P(),
            P(None, "tp"),
            P(None, "tp"),
            P("tp", None),
            P("tp"),
            P(None, None, "tp"),
            P(None, "tp"),
            P("req", None, "tp"),
            P("tp", None),
            P(None, "tp"),
            P("tp"),
            P(None, "tp"),
            P("tp"),
            P("req", None, "tp"),
            P("tp"),
            P("tp", None),
            P("req", "tp", None, None),
            P(),
            P("req"),
            P("req"),
        ),
        out_specs=(P("req", "tp"), P("req", None, "tp")),
        check_vma=False,
    )
```

profile of v0, /device:TPU:2, one launch (start us, length us, event | category | flops | bytes accessed | tf_op | source)
XLA Modules:
  0.0 191.9 jit_solution(11031688939695422736)
XLA Ops:
  8.7 0.9 multiply_reduce_fusion.3
  9.6 1.3 fusion.74
  11.9 1.7 fusion.69
  14.0 50.3 %all_gather.3 = bf16[512,320]{1,0:T(8,128)(2,1)S(1)} all-gather(bf16[8,320]{1,0:T(8,128)(2,1)S(1)} %convert_element_type.89), channel_id=1, replica_groups=mesh['req'=64,'tp'=4] {'req'}, dimensions={0}, use_global_device_ids=true | all-gather | bytes 332800 | tf_op jit(solution)/shard_map/all_gather | solution.py:73
  66.0 3.6 %fusion.73 = (f32[34,5]{1,0:T(8,128)S(1)}, f32[34,5,512]{2,1,0:T(8,128)S(1)}) fusion(bf16[34,1,512,128]{3,2,1,0:T(8,128)(2,1)} %param.38, bf16[34,5,64]{2,1,0:T(8,128)(2,1)S(1)} %gather.16, pred[34]{0:T(512)(128)(4,1)S(1)} %get-tuple-element.14, pred[34,512]{1,0:T(8,128)(4,1)S(1)} %iota_compare_fusion.1), kind=kOutput, calls=%fused_computation.108 | convolution fusion | flops 11412950 | bytes 4844490 | tf_op jit(solution)/shard_map/shd,std->sht/dot_general | solution.py:83
  71.3 0.8 copy.72
  72.1 8.1 %all-to-all-start.2 = ((f32[64,8,5]{1,2,0:T(8,128)}), f32[64,8,5]{1,2,0:T(8,128)S(1)}, u32[]{:S(2)}, u32[]{:S(2)}) async-start(f32[64,8,5]{1,2,0:T(8,128)} %copy.72), calls=%async_computation.2 | async-start | bytes 524288 | tf_op jit(solution)/shard_map/all_to_all | solution.py:113
  80.3 3.7 %fusion.20 = f32[34,5,64]{2,1,0:T(8,128)S(1)} fusion(bf16[34,1,512,128]{3,2,1,0:T(8,128)(2,1)} %param.38, f32[34,5]{1,0:T(8,128)S(1)} %subtract_exponential_fusion.1, f32[34,5,512]{2,1,0:T(8,128)S(1)} %get-tuple-element.29, f32[34,5]{1,0:T(8,128)S(1)} %get-tuple-element.28, pred[34,512]{1,0:T(8,128)(4,1)S(1)} %iota_compare_fusion.1), kind=kOutput, calls=%fused_computation.21 | convolution fusion | flops 11413120 | bytes 4866896 | tf_op jit(solution)/shard_map/sht,std->shd/dot_general | solution.py:92
  84.2 1.8 fusion.75
  86.2 10.8 %psum.22 = f32[8,132]{1,0:T(8,128)S(1)} all-reduce(f32[8,132]{1,0:T(8,128)S(1)} %fusion.77), channel_id=1, replica_groups=mesh['req'=64,'tp'=4] {'tp'}, use_global_device_ids=true, to_apply=%region_10.11 | all-reduce | flops 1056 | bytes 8448 | tf_op jit(solution)/shard_map/psum | solution.py:147
  97.1 1.4 fusion.41
  98.8 0.8 copy.67
  99.7 10.3 %all-to-all-start.1 = ((f32[64,8,5]{1,2,0:T(8,128)}), f32[64,8,5]{1,2,0:T(8,128)S(1)}, u32[]{:S(2)}, u32[]{:S(2)}) async-start(f32[64,8,5]{1,2,0:T(8,128)} %copy.67), calls=%async_computation.1 | async-start | bytes 524288 | tf_op jit(solution)/shard_map/all_to_all | solution.py:120
  110.0 0.9 multiply_reduce_fusion.1
  110.9 10.7 %all-to-all-done.1 = f32[64,8,5]{1,2,0:T(8,128)S(1)} async-done(((f32[64,8,5]{1,2,0:T(8,128)}), f32[64,8,5]{1,2,0:T(8,128)S(1)}, u32[]{:S(2)}, u32[]{:S(2)}) %all-to-all-start.1) | async-done | bytes 10272 | tf_op jit(solution)/shard_map/all_to_all | solution.py:120
  121.6 6.5 %all-to-all-start = ((f32[64,8,320]{2,1,0:T(8,128)}), f32[64,8,320]{2,1,0:T(8,128)S(1)}, u32[]{:S(2)}, u32[]{:S(2)}) async-start(f32[64,8,320]{2,1,0:T(8,128)} %fusion.41), calls=%async_computation | async-start | bytes 1572864 | tf_op jit(solution)/shard_map/all_to_all | solution.py:106
  128.3 1.9 %multiply_reduce_fusion.5 = (f32[8]{0:T(128)S(1)}, f32[8,400]{1,0:T(8,128)S(1)}) fusion(bf16[2,1600,400]{1,2,0:T(8,128)(2,1)} %param.27, f32[1600]{0:T(1024)S(1)} %copy-done.7, f32[8]{0:T(128)S(1)} %add_rsqrt_fusion, bf16[8,1600]{1,0:T(8,128)(2,1)S(1)} %copy-done.3, f32[8,400]{1,0:T(8,128)S(1)} %get-tuple-element.4, ...), kind=kOutput, calls=%fused_computation.61 | convolution fusion | flops 10323192 | bytes 1396864 | tf_op jit(solution)/shard_map/dot_general | solution.py:141
  130.6 1.4 copy.70
  132.5 17.5 %all-to-all-done = f32[64,8,320]{2,1,0:T(8,128)S(1)} async-done(((f32[64,8,320]{2,1,0:T(8,128)}), f32[64,8,320]{2,1,0:T(8,128)S(1)}, u32[]{:S(2)}, u32[]{:S(2)}) %all-to-all-start) | async-done | bytes 655392 | tf_op jit(solution)/shard_map/all_to_all | solution.py:106
  149.9 1.3 multiply_reduce_fusion
  151.4 7.7 %all-reduce = (f32[8]{0:T(128)S(1)}, f32[8]{0:T(128)S(1)}) all-reduce(f32[8]{0:T(128)S(1)} %get-tuple-element.6, f32[8]{0:T(128)S(1)} %get-tuple-element.36), channel_id=1, replica_groups=mesh['req'=64,'tp'=4] {'tp'}, use_global_device_ids=true, to_apply=%region_9.10 | all-reduce | flops 16 | bytes 128 | tf_op jit(solution)/shard_map/psum | solution.py:172
  159.7 1.2 copy.74
  160.9 22.4 %reduce-scatter.4.cloned.1.call-done = f32[400,8]{1,0:T(8,128)} async-done(((f32[1600,8]{1,0:T(8,128)}), f32[400,8]{1,0:T(8,128)}) %reduce-scatter.4.cloned.1.call-update) | async-done | bytes 12816
  183.3 1.0 copy.75
  (90 shorter events, 9.5 us)
Async XLA Ops:
  7.2 152.2 %copy-start = (bf16[400,1600]{1,0:T(8,128)(2,1)S(1)}, bf16[400,1600]{1,0:T(8,128)(2,1)}, u32[]{:S(2)}) copy-start(bf16[400,1600]{1,0:T(8,128)(2,1)} %param.37) | copy-start | bytes 3840004
  7.2 57.2 %copy-start.1 = (s32[512]{0:T(512)S(1)}, s32[512]{0:T(512)}, u32[]{:S(2)}) copy-start(s32[512]{0:T(512)} %param.39) | copy-start | bytes 6148
  11.9 54.0 %copy-start.10 = (s32[34]{0:T(128)S(1)}, s32[34]{0:T(128)}, u32[]{:S(2)}) copy-start(s32[34]{0:T(128)} %param.40) | copy-start | bytes 412
  11.9 54.0 %copy-start.14 = (s32[34]{0:T(128)S(1)}, s32[34]{0:T(128)}, u32[]{:S(2)}) copy-start(s32[34]{0:T(128)} %param.41) | copy-start | bytes 412
  72.1 27.5 %all-to-all-start.2 = ((f32[64,8,5]{1,2,0:T(8,128)}), f32[64,8,5]{1,2,0:T(8,128)S(1)}, u32[]{:S(2)}, u32[]{:S(2)}) async-start(f32[64,8,5]{1,2,0:T(8,128)} %copy.72), calls=%async_computation.2 | async-start | bytes 524288 | tf_op jit(solution)/shard_map/all_to_all | solution.py:113
  80.2 3.9 %copy-start.9 = (f32[4,400]{1,0:T(4,128)S(1)}, f32[4,400]{1,0:T(4,128)}, u32[]{:S(2)}) copy-start(f32[4,400]{1,0:T(4,128)} %param.28) | copy-start | bytes 19204
  80.3 3.9 %copy-start.3 = (bf16[8,1600]{1,0:T(8,128)(2,1)S(1)}, bf16[8,1600]{1,0:T(8,128)(2,1)}, u32[]{:S(2)}) copy-start(bf16[8,1600]{1,0:T(8,128)(2,1)} %param.21) | copy-start | bytes 76804
  80.3 3.9 %copy-start.7 = (f32[1600]{0:T(1024)S(1)}, f32[1600]{0:T(1024)}, u32[]{:S(2)}) copy-start(f32[1600]{0:T(1024)} %param.22) | copy-start | bytes 19204
  84.0 2.1 %copy-start.5 = (bf16[400,132]{0,1:T(8,128)(2,1)S(1)}, bf16[400,132]{0,1:T(8,128)(2,1)}, u32[]{:S(2)}) copy-start(bf16[400,132]{0,1:T(8,128)(2,1)} %param.30) | copy-start | bytes 316804
  84.1 14.3 %copy-start.6 = (bf16[100,400]{0,1:T(8,128)(2,1)S(1)}, bf16[100,400]{0,1:T(8,128)(2,1)}, u32[]{:S(2)}) copy-start(bf16[100,400]{0,1:T(8,128)(2,1)} %param.31) | copy-start | bytes 240004
  84.1 14.3 %copy-start.11 = (f32[400]{0:T(512)S(1)}, f32[400]{0:T(512)}, u32[]{:S(2)}) copy-start(f32[400]{0:T(512)} %param.32) | copy-start | bytes 4804
  84.2 15.5 %copy-start.8 = (f32[16,400]{1,0:T(8,128)S(1)}, f32[16,400]{1,0:T(8,128)}, u32[]{:S(2)}) copy-start(f32[16,400]{1,0:T(8,128)} %param.33) | copy-start | bytes 76804
  86.1 24.0 %copy-start.4 = (f32[8,16,400]{2,1,0:T(8,128)S(1)}, f32[8,16,400]{2,1,0:T(8,128)}, u32[]{:S(2)}) copy-start(f32[8,16,400]{2,1,0:T(8,128)} %param.35) | copy-start | bytes 614404
  99.7 28.6 %copy-start.15 = (f32[400]{0:T(512)S(1)}, f32[400]{0:T(512)}, u32[]{:S(2)}) copy-start(f32[400]{0:T(512)} %param.34) | copy-start | bytes 4804
  99.7 21.9 %all-to-all-start.1 = ((f32[64,8,5]{1,2,0:T(8,128)}), f32[64,8,5]{1,2,0:T(8,128)S(1)}, u32[]{:S(2)}, u32[]{:S(2)}) async-start(f32[64,8,5]{1,2,0:T(8,128)} %copy.67), calls=%async_computation.1 | async-start | bytes 524288 | tf_op jit(solution)/shard_map/all_to_all | solution.py:120
  121.6 28.4 %all-to-all-start = ((f32[64,8,320]{2,1,0:T(8,128)}), f32[64,8,320]{2,1,0:T(8,128)S(1)}, u32[]{:S(2)}, u32[]{:S(2)}) async-start(f32[64,8,320]{2,1,0:T(8,128)} %fusion.41), calls=%async_computation | async-start | bytes 1572864 | tf_op jit(solution)/shard_map/all_to_all | solution.py:106
  128.1 55.2 %reduce-scatter.4.cloned.1.call-start = ((), (), s32[]{:S(2)}) async-start(), calls=%async_computation.4 | async-start | bytes 1024000
  132.0 27.1 %copy-start.2 = (bf16[320,1600]{1,0:T(8,128)(2,1)S(1)}, bf16[320,1600]{1,0:T(8,128)(2,1)}, u32[]{:S(2)}) copy-start(bf16[320,1600]{1,0:T(8,128)(2,1)} %param.25) | copy-start | bytes 3072004
  132.0 27.1 %copy-start.12 = (f32[320]{0:T(512)S(1)}, f32[320]{0:T(512)}, u32[]{:S(2)}) copy-start(f32[320]{0:T(512)} %param.26) | copy-start | bytes 3844
  132.5 26.9 %copy-start.13 = (f32[400]{0:T(512)S(1)}, f32[400]{0:T(512)}, u32[]{:S(2)}) copy-start(f32[400]{0:T(512)} %param.36) | copy-start | bytes 4804
Sparse Core Ops, SparseCore 0:
  161.0 22.2 reduce-scatter.3
where the time goes:
time: 193 us; the launch traced here: 192 us
  blocking collectives  68.9 us (36%)
  waiting for transfers between devices  50.5 us (26%)
  starting transfers between devices  25 us (13%)
  matrix products  16.5 us (9%)
  between operations  14.4 us (7%)
  local copies, waits for them, and re-layouts  8.94 us (5%)
  other arithmetic  7.63 us (4%)
    all_gather x1, blocking collectives, body(): lax.all_gather(query.reshape(row_count, head_count * head_dim), 'req', ax...  50.3 us
    unnamed x2, waiting for transfers between devices  22.4 us
    all_to_all x1, waiting for transfers between devices, body(): lax.all_to_all(part_out.reshape(holders, row_count, head_count * head_dim...  17.5 us
    psum x1, blocking collectives, body(): lax.psum(jnp.dot(activated, select_weight, preferred_element_type=jnp.flo...  10.8 us
    all_to_all x1, waiting for transfers between devices, body(): lax.all_to_all(request_max.reshape(holders, row_count, head_count), 'req'...  10.7 us
    all_to_all x1, starting transfers between devices, body(): lax.all_to_all(request_max.reshape(holders, row_count, head_count), 'req'...  10.3 us
    all_to_all x1, starting transfers between devices, body(): lax.all_to_all(part_sum.reshape(holders, row_count, head_count), 'req', s...  8.09 us
    psum x1, blocking collectives, body(): attn_total, mamba_total = lax.psum((attn_square, mamba_square), 'tp')  7.74 us
  transfers between devices with their start and end apart: 4, of which 3 were waited for; matrix products, arithmetic and copies ran while one was open for 7% of the time, Pallas kernels for 0%

commit v1 on v0

--- a/solution.py
+++ b/solution.py
@@ -1,3 +1,4 @@
+import functools
 import jax
 import jax.numpy as jnp
 from jax import lax
@@ -6,6 +7,19 @@
 HQ = 20
 HD = 64
 MI = 1600
+
+
+def match_the_loops(raw, bus_axis):
+    shares = lax.axis_size(bus_axis)
+    queue = []
+    for u in range(raw.ndim):
+        queue.append(shares if u == 0 else 1)
+    plain = jnp.tile(raw, queue)
+    res = lax.all_to_all(plain, bus_axis, split_axis=0, concat_axis=0, tiled=True)
+    return res
+
+
+lift_marks = functools.partial(match_the_loops, bus_axis="req")
 
 
 def rotate_pairs(vector, position):
@@ -70,9 +84,7 @@
     memory = jnp.dot(normed, memory_weight, preferred_element_type=jnp.float32)
     key_new = rotate_pairs(memory[:, None, :head_dim], own_len).astype(jnp.bfloat16)
     value_new = memory[:, head_dim:].astype(jnp.bfloat16)
-    all_query = lax.all_gather(
-        query.reshape(row_count, head_count * head_dim), "req", axis=0, tiled=True
-    )
+    all_query = lift_marks(query.reshape(row_count, head_count * head_dim))
     slot_used = slot_request >= 0
     owner_row = jnp.where(slot_used, slot_request, 0)
     slot_query = jnp.take(all_query, owner_row, axis=0).reshape(slot_count, head_count, head_dim)

time: 193 us -> 159 us (0.82)
  blocking collectives: 68.9 us -> 18.6 us
  starting transfers between devices: 25 us -> 35.5 us
  waiting for transfers between devices: 50.5 us -> 56.8 us
    all_gather x1 -> x0, blocking collectives: 50.3 us -> none  [body(): lax.all_gather(query.reshape(row_count, head_count * head_dim), 'req', ax...]
    all_to_all x0 -> x1, starting transfers between devices: none -> 12.2 us  [match_the_loops(): lax.all_to_all(plain, bus_axis, split_axis=0, concat_axis=0, tiled=True)]
    all_to_all x1, waiting for transfers between devices: 0.01 us -> 6.8 us  [body(): lax.all_to_all(part_sum.reshape(holders, row_count, head_count), 'req', s...]
    all_to_all x1, starting transfers between devices: 10.3 us -> 6.49 us  [body(): lax.all_to_all(request_max.reshape(holders, row_count, head_count), 'req'...]
    all_to_all x1, starting transfers between devices: 8.09 us -> 10.3 us  [body(): lax.all_to_all(part_sum.reshape(holders, row_count, head_count), 'req', s...]
  transfers between devices with their start and end apart: 4 -> 5, of which waited for: 3 -> 4; matrix products, arithmetic and copies ran while one was open for 7% -> 9% of each run, Pallas kernels for 0% -> 0%
where the time goes in v1:
time: 159 us; the launch traced here: 158 us
  waiting for transfers between devices  56.8 us (36%)
  starting transfers between devices  35.5 us (22%)
  blocking collectives  18.6 us (12%)
  matrix products  16.5 us (10%)
  between operations  14.4 us (9%)
  local copies, waits for them, and re-layouts  9.73 us (6%)
  other arithmetic  6.36 us (4%)
    unnamed x2, waiting for transfers between devices  22.4 us
    all_to_all x1, waiting for transfers between devices, body(): lax.all_to_all(part_out.reshape(holders, row_count, head_count * head_dim...  17.5 us
    all_to_all x1, starting transfers between devices, match_the_loops(): lax.all_to_all(plain, bus_axis, split_axis=0, concat_axis=0, tiled=True)  12.2 us
    psum x1, blocking collectives, body(): lax.psum(jnp.dot(activated, select_weight, preferred_element_type=jnp.flo...  10.8 us
    all_to_all x1, starting transfers between devices, body(): lax.all_to_all(part_sum.reshape(holders, row_count, head_count), 'req', s...  10.3 us
    all_to_all x1, waiting for transfers between devices, body(): lax.all_to_all(request_max.reshape(holders, row_count, head_count), 'req'...  10.1 us
    psum x1, blocking collectives, body(): attn_total, mamba_total = lax.psum((attn_square, mamba_square), 'tp')  7.74 us
    all_to_all x1, waiting for transfers between devices, body(): lax.all_to_all(part_sum.reshape(holders, row_count, head_count), 'req', s...  6.8 us
  transfers between devices with their start and end apart: 5, of which 4 were waited for; matrix products, arithmetic and copies ran while one was open for 9% of the time, Pallas kernels for 0%

profile of v1, /device:TPU:2, one launch (start us, length us, event | category | flops | bytes accessed | tf_op | source)
XLA Modules:
  0.0 157.9 jit_solution(17377567592609342714)
XLA Ops:
  7.2 1.0 multiply_reduce_fusion.3
  8.2 1.3 fusion.74
  9.5 0.8 dynamic-slice_convert_fusion
  10.6 1.7 %fusion.69 = f32[8,320]{1,0:T(8,128)S(1)} fusion(bf16[1600,320]{0,1:T(8,128)(2,1)} %param.23, f32[1600]{0:T(1024)} %param.22, f32[8]{0:T(128)S(1)} %add_rsqrt_fusion, bf16[8,1600]{1,0:T(8,128)(2,1)} %param.21), kind=kOutput, calls=%fused_computation.104 | convolution fusion | flops 8243200 | bytes 1066272 | tf_op jit(solution)/shard_map/dot_general | solution.py:80
  13.5 12.2 %all-to-all-start = ((bf16[64,8,320]{2,1,0:T(8,128)(2,1)}), bf16[64,8,320]{2,1,0:T(8,128)(2,1)S(1)}, u32[]{:S(2)}, u32[]{:S(2)}) async-start(bf16[64,8,320]{2,1,0:T(8,128)(2,1)} %tile.2), calls=%async_computation | async-start | bytes 786432 | tf_op jit(solution)/shard_map/all_to_all | solution.py:18
  26.8 1.8 %fusion.75 = (f32[8,400]{1,0:T(8,128)S(1)}, bf16[8,400]{1,0:T(8,128)(2,1)S(1)}) fusion(bf16[8,3,400]{2,0,1:T(8,128)(2,1)} %param.29, f32[400]{0:T(512)S(1)} %bitcast.83, f32[400]{0:T(512)S(1)} %bitcast.84, f32[400]{0:T(512)S(1)} %bitcast.82, bf16[2,1600,400]{1,2,0:T(8,128)(2,1)} %param.27, f32[1600]{0:T(1024)S(1)} %copy-done.7, f32[8]{0:T(128)S(1)} %add_rsqrt_fusion, ...), kind=kOutput, calls=%fused_computation.110 | convolution fusion | flops 10348800 | bytes 1413408 | tf_op jit(solution)/shard_map/dot_general | solution.py:150
  28.8 10.8 %psum.22 = f32[8,132]{1,0:T(8,128)S(1)} all-reduce(f32[8,132]{1,0:T(8,128)S(1)} %fusion.77), channel_id=1, replica_groups=mesh['req'=64,'tp'=4] {'tp'}, use_global_device_ids=true, to_apply=%region_10.11 | all-reduce | flops 1056 | bytes 8448 | tf_op jit(solution)/shard_map/psum | solution.py:159
  40.0 0.9 multiply_reduce_fusion.1
  41.6 3.6 %fusion.73 = (f32[34,5]{1,0:T(8,128)S(1)}, f32[34,5,512]{2,1,0:T(8,128)S(1)}) fusion(bf16[34,1,512,128]{3,2,1,0:T(8,128)(2,1)} %param.38, bf16[34,5,64]{2,1,0:T(8,128)(2,1)S(1)} %gather.16, pred[34]{0:T(512)(128)(4,1)S(1)} %get-tuple-element.14, pred[34,512]{1,0:T(8,128)(4,1)S(1)} %iota_compare_fusion.1), kind=kOutput, calls=%fused_computation.108 | convolution fusion | flops 11412950 | bytes 4844490 | tf_op jit(solution)/shard_map/shd,std->sht/dot_general | solution.py:95
  47.7 10.3 %all-to-all-start.3 = ((f32[64,8,5]{1,2,0:T(8,128)}), f32[64,8,5]{1,2,0:T(8,128)S(1)}, u32[]{:S(2)}, u32[]{:S(2)}) async-start(f32[64,8,5]{1,2,0:T(8,128)} %copy.72), calls=%async_computation.3 | async-start | bytes 524288 | tf_op jit(solution)/shard_map/all_to_all | solution.py:125
  58.1 3.7 %fusion.20 = f32[34,5,64]{2,1,0:T(8,128)S(1)} fusion(bf16[34,1,512,128]{3,2,1,0:T(8,128)(2,1)} %param.38, f32[34,5]{1,0:T(8,128)S(1)} %subtract_exponential_fusion.1, f32[34,5,512]{2,1,0:T(8,128)S(1)} %get-tuple-element.29, f32[34,5]{1,0:T(8,128)S(1)} %get-tuple-element.28, pred[34,512]{1,0:T(8,128)(4,1)S(1)} %iota_compare_fusion.1), kind=kOutput, calls=%fused_computation.21 | convolution fusion | flops 11413120 | bytes 4866896 | tf_op jit(solution)/shard_map/sht,std->shd/dot_general | solution.py:104
  62.8 6.8 %all-to-all-done.3 = f32[64,8,5]{1,2,0:T(8,128)S(1)} async-done(((f32[64,8,5]{1,2,0:T(8,128)}), f32[64,8,5]{1,2,0:T(8,128)S(1)}, u32[]{:S(2)}, u32[]{:S(2)}) %all-to-all-start.3) | async-done | bytes 10272 | tf_op jit(solution)/shard_map/all_to_all | solution.py:125
  69.6 6.5 %all-to-all-start.2 = ((f32[64,8,5]{1,2,0:T(8,128)}), f32[64,8,5]{1,2,0:T(8,128)S(1)}, u32[]{:S(2)}, u32[]{:S(2)}) async-start(f32[64,8,5]{1,2,0:T(8,128)} %copy.67), calls=%async_computation.2 | async-start | bytes 524288 | tf_op jit(solution)/shard_map/all_to_all | solution.py:132
  76.1 1.4 fusion.41
  77.5 10.1 %all-to-all-done.2 = f32[64,8,5]{1,2,0:T(8,128)S(1)} async-done(((f32[64,8,5]{1,2,0:T(8,128)}), f32[64,8,5]{1,2,0:T(8,128)S(1)}, u32[]{:S(2)}, u32[]{:S(2)}) %all-to-all-start.2) | async-done | bytes 10272 | tf_op jit(solution)/shard_map/all_to_all | solution.py:132
  87.6 6.5 %all-to-all-start.1 = ((f32[64,8,320]{2,1,0:T(8,128)}), f32[64,8,320]{2,1,0:T(8,128)S(1)}, u32[]{:S(2)}, u32[]{:S(2)}) async-start(f32[64,8,320]{2,1,0:T(8,128)} %fusion.41), calls=%async_computation.1 | async-start | bytes 1572864 | tf_op jit(solution)/shard_map/all_to_all | solution.py:118
  94.3 1.9 %multiply_reduce_fusion.5 = (f32[8]{0:T(128)S(1)}, f32[8,400]{1,0:T(8,128)S(1)}) fusion(bf16[2,1600,400]{1,2,0:T(8,128)(2,1)} %param.27, f32[1600]{0:T(1024)S(1)} %copy-done.7, f32[8]{0:T(128)S(1)} %add_rsqrt_fusion, bf16[8,1600]{1,0:T(8,128)(2,1)S(1)} %copy-done.3, f32[8,400]{1,0:T(8,128)S(1)} %get-tuple-element.4, ...), kind=kOutput, calls=%fused_computation.61 | convolution fusion | flops 10323192 | bytes 1396864 | tf_op jit(solution)/shard_map/dot_general | solution.py:153
  96.7 1.4 copy.70
  98.5 17.5 %all-to-all-done.1 = f32[64,8,320]{2,1,0:T(8,128)S(1)} async-done(((f32[64,8,320]{2,1,0:T(8,128)}), f32[64,8,320]{2,1,0:T(8,128)S(1)}, u32[]{:S(2)}, u32[]{:S(2)}) %all-to-all-start.1) | async-done | bytes 655392 | tf_op jit(solution)/shard_map/all_to_all | solution.py:118
  116.0 1.3 multiply_reduce_fusion
  117.4 7.7 %all-reduce = (f32[8]{0:T(128)S(1)}, f32[8]{0:T(128)S(1)}) all-reduce(f32[8]{0:T(128)S(1)} %get-tuple-element.6, f32[8]{0:T(128)S(1)} %get-tuple-element.36), channel_id=1, replica_groups=mesh['req'=64,'tp'=4] {'tp'}, use_global_device_ids=true, to_apply=%region_9.10 | all-reduce | flops 16 | bytes 128 | tf_op jit(solution)/shard_map/psum | solution.py:184
  125.7 1.2 copy.74
  127.0 22.4 %reduce-scatter.4.cloned.1.call-done = f32[400,8]{1,0:T(8,128)} async-done(((f32[1600,8]{1,0:T(8,128)}), f32[400,8]{1,0:T(8,128)}) %reduce-scatter.4.cloned.1.call-update) | async-done | bytes 12816
  149.4 1.0 copy.75
  (92 shorter events, 9.7 us)
Async XLA Ops:
  7.2 118.3 %copy-start = (bf16[400,1600]{1,0:T(8,128)(2,1)S(1)}, bf16[400,1600]{1,0:T(8,128)(2,1)}, u32[]{:S(2)}) copy-start(bf16[400,1600]{1,0:T(8,128)(2,1)} %param.37) | copy-start | bytes 3840004
  9.4 16.3 %copy-start.10 = (s32[34]{0:T(128)S(1)}, s32[34]{0:T(128)}, u32[]{:S(2)}) copy-start(s32[34]{0:T(128)} %param.40) | copy-start | bytes 412
  9.4 16.4 %copy-start.1 = (s32[512]{0:T(512)S(1)}, s32[512]{0:T(512)}, u32[]{:S(2)}) copy-start(s32[512]{0:T(512)} %param.39) | copy-start | bytes 6148
  10.5 16.2 %copy-start.14 = (s32[34]{0:T(128)S(1)}, s32[34]{0:T(128)}, u32[]{:S(2)}) copy-start(s32[34]{0:T(128)} %param.41) | copy-start | bytes 412
  10.5 16.3 %copy-start.9 = (f32[4,400]{1,0:T(4,128)S(1)}, f32[4,400]{1,0:T(4,128)}, u32[]{:S(2)}) copy-start(f32[4,400]{1,0:T(4,128)} %param.28) | copy-start | bytes 19204
  10.5 16.3 %copy-start.3 = (bf16[8,1600]{1,0:T(8,128)(2,1)S(1)}, bf16[8,1600]{1,0:T(8,128)(2,1)}, u32[]{:S(2)}) copy-start(bf16[8,1600]{1,0:T(8,128)(2,1)} %param.21) | copy-start | bytes 76804
  10.5 16.3 %copy-start.7 = (f32[1600]{0:T(1024)S(1)}, f32[1600]{0:T(1024)}, u32[]{:S(2)}) copy-start(f32[1600]{0:T(1024)} %param.22) | copy-start | bytes 19204
  13.5 15.2 %copy-start.5 = (bf16[400,132]{0,1:T(8,128)(2,1)S(1)}, bf16[400,132]{0,1:T(8,128)(2,1)}, u32[]{:S(2)}) copy-start(bf16[400,132]{0,1:T(8,128)(2,1)} %param.30) | copy-start | bytes 316804
  13.5 27.3 %all-to-all-start = ((bf16[64,8,320]{2,1,0:T(8,128)(2,1)}), bf16[64,8,320]{2,1,0:T(8,128)(2,1)S(1)}, u32[]{:S(2)}, u32[]{:S(2)}) async-start(bf16[64,8,320]{2,1,0:T(8,128)(2,1)} %tile.2), calls=%async_computation | async-start | bytes 786432 | tf_op jit(solution)/shard_map/all_to_all | solution.py:18
  25.7 14.0 %copy-start.8 = (f32[16,400]{1,0:T(8,128)S(1)}, f32[16,400]{1,0:T(8,128)}, u32[]{:S(2)}) copy-start(f32[16,400]{1,0:T(8,128)} %param.33) | copy-start | bytes 76804
  25.7 14.1 %copy-start.6 = (bf16[100,400]{0,1:T(8,128)(2,1)S(1)}, bf16[100,400]{0,1:T(8,128)(2,1)}, u32[]{:S(2)}) copy-start(bf16[100,400]{0,1:T(8,128)(2,1)} %param.31) | copy-start | bytes 240004
  25.7 14.1 %copy-start.11 = (f32[400]{0:T(512)S(1)}, f32[400]{0:T(512)}, u32[]{:S(2)}) copy-start(f32[400]{0:T(512)} %param.32) | copy-start | bytes 4804
  25.7 14.2 %copy-start.4 = (f32[8,16,400]{2,1,0:T(8,128)S(1)}, f32[8,16,400]{2,1,0:T(8,128)}, u32[]{:S(2)}) copy-start(f32[8,16,400]{2,1,0:T(8,128)} %param.35) | copy-start | bytes 614404
  47.7 21.9 %all-to-all-start.3 = ((f32[64,8,5]{1,2,0:T(8,128)}), f32[64,8,5]{1,2,0:T(8,128)S(1)}, u32[]{:S(2)}, u32[]{:S(2)}) async-start(f32[64,8,5]{1,2,0:T(8,128)} %copy.72), calls=%async_computation.3 | async-start | bytes 524288 | tf_op jit(solution)/shard_map/all_to_all | solution.py:125
  69.6 18.0 %all-to-all-start.2 = ((f32[64,8,5]{1,2,0:T(8,128)}), f32[64,8,5]{1,2,0:T(8,128)S(1)}, u32[]{:S(2)}, u32[]{:S(2)}) async-start(f32[64,8,5]{1,2,0:T(8,128)} %copy.67), calls=%async_computation.2 | async-start | bytes 524288 | tf_op jit(solution)/shard_map/all_to_all | solution.py:132
  76.1 18.2 %copy-start.15 = (f32[400]{0:T(512)S(1)}, f32[400]{0:T(512)}, u32[]{:S(2)}) copy-start(f32[400]{0:T(512)} %param.34) | copy-start | bytes 4804
  87.6 28.4 %all-to-all-start.1 = ((f32[64,8,320]{2,1,0:T(8,128)}), f32[64,8,320]{2,1,0:T(8,128)S(1)}, u32[]{:S(2)}, u32[]{:S(2)}) async-start(f32[64,8,320]{2,1,0:T(8,128)} %fusion.41), calls=%async_computation.1 | async-start | bytes 1572864 | tf_op jit(solution)/shard_map/all_to_all | solution.py:118
  94.1 55.2 %reduce-scatter.4.cloned.1.call-start = ((), (), s32[]{:S(2)}) async-start(), calls=%async_computation.5 | async-start | bytes 1024000
  98.0 27.1 %copy-start.2 = (bf16[320,1600]{1,0:T(8,128)(2,1)S(1)}, bf16[320,1600]{1,0:T(8,128)(2,1)}, u32[]{:S(2)}) copy-start(bf16[320,1600]{1,0:T(8,128)(2,1)} %param.25) | copy-start | bytes 3072004
  98.0 27.1 %copy-start.12 = (f32[320]{0:T(512)S(1)}, f32[320]{0:T(512)}, u32[]{:S(2)}) copy-start(f32[320]{0:T(512)} %param.26) | copy-start | bytes 3844
  98.5 26.9 %copy-start.13 = (f32[400]{0:T(512)S(1)}, f32[400]{0:T(512)}, u32[]{:S(2)}) copy-start(f32[400]{0:T(512)} %param.36) | copy-start | bytes 4804
Sparse Core Ops, SparseCore 0:
  127.1 22.2 reduce-scatter.3
